TPU v7x, 512 devices: a whole 4x8x8 slice. The times are simulated.
512 devices in a mesh: seq: 128 (over z, y, core), tensor: 4 (over x).
Axes of the slice: x: 4, y: 8, z: 8, core: 2. Of those that a mesh axis runs over, the one named last changes fastest.
Arguments:
- query: bfloat16 [128, 3072], P('seq', 'tensor'), may hold values from -6 to 6
- page_owner: int32 [2048], P('seq'), may hold values from 0 to 127, as said below
- page_fill: int32 [2048], P('seq'), may hold values from 0 to 64, as said below
- cache: bfloat16 [2048, 64, 576], P('seq'), may hold values from -32 to 32
- w_uk: bfloat16 [16, 128, 512], P('tensor'), may hold values from -0.5 to 0.5
- w_uv: bfloat16 [16, 512, 128], P('tensor'), may hold values from -0.25 to 0.25
- w_out: bfloat16 [2048, 2048], P('tensor'), may hold values from -0.125 to 0.125
Outputs:
- attn_out: bfloat16 [128, 2048], P('seq', 'tensor')
Inputs may be any that keep to these rules, and one draw needn't show every extreme that they name: `page_owner`: slots with page_fill 0 are unused and name request 0; every request has at least one page with page_fill 1 or more; a device's used slots come first among its 16; some device uses all 16. `page_fill`: the first slot of every device is full.
All inputs are finite; a program needn't handle non-finite values.
Results may differ from a plain program's by a relative error of at most 0.014.
Values may be sent and summed in bfloat16 or wider, within the bound.
A program may use at most 64 MiB of HBM per device.

v0:
```python
import math

import jax
import jax.numpy as jnp
from jax import lax
from jax.sharding import PartitionSpec as P


def absorb(rows, w_uk):
    heads_here, nope_width, latent = w_uk.shape
    shaped = rows.reshape(rows.shape[0], heads_here, -1)
    latent_q = jnp.einsum(
        "rhn,hnc->rhc", shaped[:, :, :nope_width], w_uk, preferred_element_type=jnp.float32
    ).astype(jnp.bfloat16)
    return jnp.concatenate([latent_q, shaped[:, :, nope_width:]], axis=2)


def shards(query, page_owner, page_fill, cache, w_uk, w_uv, w_out):
    heads_here, nope_width, latent = w_uk.shape
    width = query.shape[1] // heads_here
    own_rows = query.shape[0]
    softmax_scale = 1.0 / math.sqrt(width)
    gathered = lax.all_gather(query, "seq", axis=0, tiled=True)
    joined = absorb(gathered, w_uk)
    requests = joined.shape[0]
    page_queries = jnp.take(joined, page_owner, axis=0)
    scores = (
        jnp.einsum("phc,ptc->pht", page_queries, cache, preferred_element_type=jnp.float32)
        * softmax_scale
    )
    usable = jnp.arange(cache.shape[1])[None, None, :] < page_fill[:, None, None]
    scores = jnp.where(usable, scores, -1e30)
    page_peak = jnp.max(scores, axis=2)
    member = page_owner[None, :] == jnp.arange(requests)[:, None]
    local_peak = jnp.max(jnp.where(member[:, :, None], page_peak[None], -1e30), axis=1)
    peak_score = lax.pmax(local_peak, "seq")
    weights = jnp.where(
        usable, jnp.exp(scores - jnp.take(peak_score, page_owner, axis=0)[:, :, None]), 0.0
    )
    totals = jnp.sum(weights, axis=2)
    values = jnp.einsum(
        "pht,ptc->phc",
        weights.astype(jnp.bfloat16),
        cache[:, :, :latent],
        preferred_element_type=jnp.float32,
    )
    member_f = member.astype(jnp.float32)
    denominator = jnp.dot(member_f, totals, precision=lax.Precision.HIGHEST)
    numerator = jnp.einsum("rp,phc->rhc", member_f, values, precision=lax.Precision.HIGHEST)
    denom_own, numer_own = (
        lax.psum_scatter(denominator, "seq", scatter_dimension=0, tiled=True),
        lax.psum_scatter(numerator, "seq", scatter_dimension=0, tiled=True),
    )
    attended = (numer_own / denom_own[:, :, None]).astype(jnp.bfloat16)
    head_out = jnp.einsum(
        "rhc,hcv->rhv", attended, w_uv, preferred_element_type=jnp.float32
    ).astype(jnp.bfloat16)
    head_out = head_out.reshape(own_rows, -1)
    partial_value = jnp.dot(head_out, w_out, preferred_element_type=jnp.float32)
    return lax.psum_scatter(partial_value, "tensor", scatter_dimension=1, tiled=True).astype(
        jnp.bfloat16
    )


def solution(mesh):
    return jax.shard_map(
        shards,
        mesh=mesh,
        in_specs=(
            P("seq", "tensor"),
            P("seq"),
            P("seq"),
            P("seq", None, None),
            P("tensor", None, None),
            P("tensor", None, None),
            P("tensor", None),
        ),
        out_specs=P("seq", "tensor"),
        check_vma=False,
    )
```

profile of v0, /device:TPU:1, one launch (start us, length us, event | category | flops | bytes accessed | tf_op | source)
XLA Modules:
  0.0 1097.0 jit_solution(8661672578728302643)
XLA Ops:
  6.5 0.0 copy-start
  6.5 0.0 copy-start.2
  6.5 0.0 all-reduce.4.cloned.1.call-start
  6.5 0.8 compare_and_fusion
  7.4 0.7 compare_select_fusion
  8.0 0.7 iota_compare_fusion.1
  8.7 0.7 iota_compare_fusion
  9.5 58.9 %all-gather = bf16[128,1,768]{2,1,0:T(2,128)(2,1)S(1)} all-gather(bf16[1,1,768]{2,1,0:T(2,128)(2,1)} %bitcast.31), channel_id=1, replica_groups=mesh['seq'=128,'tensor'=4] {'seq'}, dimensions={0}, use_global_device_ids=true | all-gather | bytes 198144 | tf_op jit(solution)/shard_map/all_gather | solution.py:23
  68.3 0.4 copy.32
  68.8 0.0 copy-done.2
  68.8 0.3 fusion
  69.1 0.0 copy-start.1
  69.1 0.9 pad_maximum_fusion
  70.0 2.1 copy.35
  72.1 1.7 gather_fusion
  73.9 0.0 copy-done.1
  73.9 0.0 copy-start.4
  73.9 0.6 fusion.27
  74.5 0.1 copy.36
  74.6 0.1 select_reduce_fusion
  74.7 0.7 copy.37
  75.5 487.8 %pmax.7 = f32[128,4]{1,0:T(8,128)S(1)} all-reduce(f32[128,4]{1,0:T(8,128)} %copy.37), channel_id=1, replica_groups=mesh['seq'=128,'tensor'=4] {'seq'}, use_global_device_ids=true, to_apply=%region_2.3 | all-reduce | flops 512 | bytes 4096 | tf_op jit(solution)/shard_map/pmax | solution.py:36
  563.3 0.6 gather_fusion.1
  563.9 0.1 broadcast_select_fusion
  563.9 0.3 fusion.2
  564.3 0.0 copy-done.4
  564.3 0.7 fusion.5
  565.0 0.0 copy-start.3
  565.0 1.7 copy.39
  566.7 0.0 all-reduce.4.cloned.1.call-update
  566.7 0.0 reduce-scatter.4.cloned.1.call-start
  566.8 1.3 dynamic-slice
  568.0 0.2 fusion.10
  568.2 0.3 fusion.20
  568.5 491.0 %all-reduce.1 = f32[128,4]{1,0:T(8,128)S(1)} all-reduce(f32[128,4]{1,0:T(8,128)S(1)} %fusion.20), channel_id=3, replica_groups=mesh['seq'=128,'tensor'=4] {'seq'}, use_global_device_ids=true, to_apply=%region_5.6.clone | all-reduce | flops 512 | bytes 4096
  1059.5 0.7 fusion.24
  1060.1 0.0 all-reduce.4.cloned.1.call-done
  1060.2 1.4 fusion.23
  1061.6 0.0 copy-done.3
  1061.6 0.2 fusion.16
  1061.8 0.0 copy-done
  1061.8 1.9 convolution_bitcast_fusion
  1063.7 0.0 reduce-scatter.4.cloned.1.call-update
  1063.7 24.8 %reduce-scatter.4.cloned.1.call-done = f32[512,1]{1,0:T(8,128)} async-done(((f32[2048,1]{1,0:T(8,128)}), f32[512,1]{1,0:T(8,128)}) %reduce-scatter.4.cloned.1.call-update) | async-done | bytes 2064
  1088.5 1.6 copy.44
  (4 shorter events, 0.0 us)
Async XLA Ops:
  6.5 1055.3 %copy-start = (bf16[512,2048]{1,0:T(8,128)(2,1)S(1)}, bf16[512,2048]{1,0:T(8,128)(2,1)}, u32[]{:S(2)}) copy-start(bf16[512,2048]{1,0:T(8,128)(2,1)} %param.13) | copy-start | bytes 6291460
  6.5 62.2 %copy-start.2 = (bf16[4,128,512]{2,1,0:T(8,128)(2,1)S(1)}, bf16[4,128,512]{2,1,0:T(8,128)(2,1)}, u32[]{:S(2)}) copy-start(bf16[4,128,512]{2,1,0:T(8,128)(2,1)} %param.11) | copy-start | bytes 1572868
  6.5 1053.6 %all-reduce.4.cloned.1.call-start = ((), (), s32[]{:S(2)}) async-start(), calls=%async_computation.2 | async-start | bytes 2097152
  69.1 4.7 copy-start.1
  73.9 490.4 %copy-start.4 = (s32[16]{0:T(128)S(1)}, s32[16]{0:T(128)}, u32[]{:S(2)}) copy-start(s32[16]{0:T(128)} %param.8) | copy-start | bytes 196
  565.0 496.6 %copy-start.3 = (bf16[4,512,128]{2,1,0:T(8,128)(2,1)S(1)}, bf16[4,512,128]{2,1,0:T(8,128)(2,1)}, u32[]{:S(2)}) copy-start(bf16[4,512,128]{2,1,0:T(8,128)(2,1)} %param.12) | copy-start | bytes 1572868
  566.7 521.8 %reduce-scatter.4.cloned.1.call-start = ((), (), s32[]{:S(2)}) async-start(), calls=%async_computation.1 | async-start | bytes 1310720
Sparse Core Ops, SparseCore 0:
  566.8 193.3 all-reduce.3
  1063.9 24.6 reduce-scatter.3
where the time goes:
time: 1100 us
  blocking collectives  1040 us (95%)
  waiting for transfers between devices  24.8 us (2%)
  between operations  13.5 us (1%)
  local copies, waits for them, and re-layouts  11 us (1%)
    unnamed x1, blocking collectives  491 us
    pmax x1, blocking collectives, shards(): peak_score = lax.pmax(local_peak, 'seq')  488 us
    all_gather x1, blocking collectives, shards(): gathered = lax.all_gather(query, 'seq', axis=0, tiled=True)  58.9 us
    unnamed x4, waiting for transfers between devices  24.8 us
  transfers between devices with their start and end apart: 2, of which 1 were waited for; matrix products, arithmetic and copies ran while one was open for 0% of the time, Pallas kernels for 0%

commit v1 on v0

v1 whole, which is shorter than its diff:
```python
import math

import jax
import jax.numpy as jnp
from jax import lax
from jax.experimental import pallas as pl
from jax.experimental.pallas import tpu as pltpu
from jax.sharding import PartitionSpec as P

MESH = pl.DeviceIdType.MESH
EMPTY = -1e30
LANES = 128
ROWS = 8
SENT = 6


def kernel(
    seq, tensor, scale,
    owner, fill, q_ref, cache_hbm, wuk_hbm, wuv_hbm, wout_hbm,
    out_ref,
    qall, cache, wuk, wuv, wout, sel, pick, sendb, recvb, rf, xs, xr,
    local_sems, qsend, qrecv, bsend, brecv, xsend, xrecv,
):
    pages, page, width = cache.shape
    heads, nope, latent = wuk.shape
    rope = width - latent
    tokens = pages * page
    me = lax.axis_index("seq")
    tx = lax.axis_index("tensor")
    barrier = pltpu.get_barrier_semaphore()

    def greet(k, c):
        pl.semaphore_signal(
            barrier, 1, device_id={"seq": lax.rem(me + k, seq)}, device_id_type=MESH
        )
        return c

    lax.fori_loop(1, seq, greet, 0)
    for k in range(1, tensor):
        pl.semaphore_signal(
            barrier, 1, device_id={"tensor": lax.rem(tx + k, tensor)}, device_id_type=MESH
        )
    loads = [
        pltpu.make_async_copy(src, dst, local_sems.at[i])
        for i, (src, dst) in enumerate(
            ((wuk_hbm, wuk), (cache_hbm, cache), (wuv_hbm, wuv), (wout_hbm, wout))
        )
    ]
    for load in loads:
        load.start()

    q = q_ref[...].astype(jnp.float32)
    step = nope + rope
    rows = [q[:, h * step : h * step + nope] for h in range(heads)]
    ropes = [q[:, h * step + nope : (h + 1) * step] for h in range(heads)]
    rows += [jnp.concatenate(ropes[h : h + 2], axis=1) for h in range(0, heads, 2)]
    rows += [jnp.zeros((ROWS - SENT, LANES), jnp.float32)]
    qall[me] = jnp.concatenate(rows, axis=0).astype(jnp.bfloat16)

    pl.semaphore_wait(barrier, seq - 1 + tensor - 1)

    def send_query(k, c):
        pltpu.make_async_remote_copy(
            src_ref=qall.at[me, pl.ds(0, SENT)],
            dst_ref=qall.at[me, pl.ds(0, SENT)],
            send_sem=qsend,
            recv_sem=qrecv,
            device_id={"seq": lax.rem(me + k, seq)},
            device_id_type=MESH,
        ).start()
        return c

    lax.fori_loop(1, seq, send_query, 0)

    row16 = lax.broadcasted_iota(jnp.int32, (pages, LANES), 0)
    lane16 = lax.broadcasted_iota(jnp.int32, (pages, LANES), 1)
    own_row = jnp.zeros((pages, LANES), jnp.int32)
    own_lane = jnp.zeros((pages, LANES), jnp.int32)
    for p in range(pages):
        own_row = jnp.where(row16 == p, owner[p], own_row)
        own_lane = jnp.where((lane16 & (pages - 1)) == p, owner[p], own_lane)
    repeated = jnp.max(
        jnp.where((own_row == own_lane) & (row16 < (lane16 & (pages - 1))), 1, 0),
        axis=0, keepdims=True,
    )
    first_lane = jnp.where(repeated > 0, -1, own_lane[:1])
    big_row = lax.broadcasted_iota(jnp.int32, (seq * ROWS, LANES), 0)
    big_lane = lax.broadcasted_iota(jnp.int32, (seq * ROWS, LANES), 1)
    wanted = (first_lane * ROWS) + lax.div(big_lane[:1], pages)
    wanted = jnp.where((first_lane >= 0) & (big_lane[:1] < (heads + 1) * pages), wanted, -1)
    pick[...] = jnp.where(big_row == wanted, 1.0, 0.0).astype(jnp.bfloat16)

    pltpu.make_async_copy(
        qall.at[pl.ds(0, seq - 1), pl.ds(0, SENT)],
        qall.at[pl.ds(0, seq - 1), pl.ds(0, SENT)],
        qrecv,
    ).wait()
    for p in range(pages):
        sel[p * ROWS : (p + 1) * ROWS, :] = qall[owner[p]].astype(jnp.float32)
    loads[0].wait()
    joined = []
    for h in range(heads):
        plain = sel[pl.ds(h, pages, stride=ROWS), :].astype(jnp.bfloat16)
        pair = sel[pl.ds(heads + h // 2, pages, stride=ROWS), :]
        turned = pair[:, (h % 2) * rope : (h % 2 + 1) * rope].astype(jnp.bfloat16)
        lat = jnp.dot(plain, wuk[h], preferred_element_type=jnp.float32).astype(jnp.bfloat16)
        joined.append(jnp.concatenate([lat, turned], axis=1))
    joined = jnp.concatenate(joined, axis=0)

    loads[1].wait()
    keys = cache[...].reshape(tokens, width)
    scores = lax.dot_general(
        joined, keys, (((1,), (1,)), ((), ())), preferred_element_type=jnp.float32
    )
    own_rows = jnp.concatenate([own_row] * heads, axis=0)
    lane = lax.broadcasted_iota(jnp.int32, (1, LANES), 1)
    per = LANES // page
    valid, kept = [], []
    for j in range(tokens // LANES):
        own_l = jnp.where(lane < page, owner[per * j], owner[per * j + 1])
        fill_l = jnp.where(lane < page, fill[per * j], fill[per * j + 1])
        own_l = jnp.where((lane & (page - 1)) < fill_l, own_l, -1)
        ok = own_rows == own_l
        valid.append(ok)
        kept.append(jnp.where(ok, scores[:, j * LANES : (j + 1) * LANES] * scale, EMPTY))
    top = kept[0]
    for part in kept[1:]:
        top = jnp.maximum(top, part)
    top = jnp.max(top, axis=1, keepdims=True)
    top = jnp.where(top > 0.5 * EMPTY, top, 0.0)
    top_hi = top.astype(jnp.bfloat16).astype(jnp.float32)
    top_lo = (top - top_hi).astype(jnp.bfloat16).astype(jnp.float32)
    shift = top_hi + top_lo
    weights = [jnp.where(ok, jnp.exp(s - shift), 0.0) for ok, s in zip(valid, kept)]
    total = weights[0]
    for part in weights[1:]:
        total = total + part
    total = jnp.sum(total, axis=1, keepdims=True)
    total_hi = total.astype(jnp.bfloat16).astype(jnp.float32)
    total_lo = total - total_hi
    weights = jnp.concatenate([w.astype(jnp.bfloat16) for w in weights], axis=1)
    sums = jnp.dot(weights, keys[:, :latent], preferred_element_type=jnp.float32)

    loads[2].wait()
    blocks = [
        jnp.dot(
            sums[h * pages : (h + 1) * pages].astype(jnp.bfloat16), wuv[h],
            preferred_element_type=jnp.float32,
        )
        for h in range(heads)
    ]
    stats = jnp.zeros((pages, LANES), jnp.float32)
    for i, part in enumerate((top_hi, top_lo, total_hi, total_lo)):
        for h in range(heads):
            stats = jnp.where(
                lane16 == i * heads + h, part[h * pages : (h + 1) * pages], stats
            )
    blocks += [stats, jnp.zeros((LANES - (heads + 1) * pages, LANES), jnp.float32)]
    table = jnp.concatenate(blocks, axis=0).astype(jnp.bfloat16)
    sendb[...] = (
        jnp.dot(pick[...], table, preferred_element_type=jnp.float32)
        .astype(jnp.bfloat16)
        .reshape(seq, ROWS, LANES)
    )
    recvb[me] = sendb[me]

    def send_sums(k, c):
        peer = lax.rem(me + k, seq)
        pltpu.make_async_remote_copy(
            src_ref=sendb.at[peer, pl.ds(0, SENT)],
            dst_ref=recvb.at[me, pl.ds(0, SENT)],
            send_sem=bsend,
            recv_sem=brecv,
            device_id={"seq": peer},
            device_id_type=MESH,
        ).start()
        return c

    lax.fori_loop(1, seq, send_sums, 0)
    pltpu.make_async_copy(
        recvb.at[pl.ds(0, seq - 1), pl.ds(0, SENT)],
        recvb.at[pl.ds(0, seq - 1), pl.ds(0, SENT)],
        brecv,
    ).wait()

    rf[...] = recvb[...].reshape(seq * ROWS, LANES).astype(jnp.float32)
    got = rf[pl.ds(heads, seq, stride=ROWS), :]
    tops = got + pltpu.roll(got, LANES - heads, 1)
    totals = pltpu.roll(got, LANES - 2 * heads, 1) + pltpu.roll(got, LANES - 3 * heads, 1)
    some = totals > 0.0
    tops = jnp.where(some, tops, EMPTY)
    peak = jnp.max(tops, axis=0, keepdims=True)
    share = jnp.where(some, jnp.exp(tops - peak), 0.0)
    denominator = jnp.sum(jnp.where(some, share * totals, 0.0), axis=0, keepdims=True)
    outs = []
    for h in range(heads):
        mine = rf[pl.ds(h, seq, stride=ROWS), :]
        numerator = jnp.sum(mine * share[:, h : h + 1], axis=0, keepdims=True)
        outs.append(numerator / denominator[:, h : h + 1])
    head_out = jnp.concatenate(outs, axis=1).astype(jnp.bfloat16)

    loads[3].wait()
    partial_value = jnp.dot(head_out, wout[...], preferred_element_type=jnp.float32)
    columns = partial_value.shape[1] // tensor
    for t in range(tensor):
        xs[t] = partial_value[:, t * columns : (t + 1) * columns]
    xr[tx] = xs[tx]
    sends = []
    for k in range(1, tensor):
        peer = lax.rem(tx + k, tensor)
        sends.append(
            pltpu.make_async_remote_copy(
                src_ref=xs.at[peer],
                dst_ref=xr.at[tx],
                send_sem=xsend.at[k],
                recv_sem=xrecv.at[k],
                device_id={"tensor": peer},
                device_id_type=MESH,
            )
        )
    for send in sends:
        send.start()
    for send in sends:
        send.wait_recv()
    total_value = xr[0]
    for t in range(1, tensor):
        total_value = total_value + xr[t]
    out_ref[...] = total_value.astype(out_ref.dtype)
    for send in sends:
        send.wait_send()
    for ref, sem in ((qall, qsend), (sendb, bsend)):
        pltpu.make_async_copy(
            ref.at[pl.ds(0, seq - 1), pl.ds(0, SENT)],
            ref.at[pl.ds(0, seq - 1), pl.ds(0, SENT)],
            sem,
        ).wait()


def solution(mesh):
    seq, tensor = mesh.shape["seq"], mesh.shape["tensor"]

    def shards(query, page_owner, page_fill, cache, w_uk, w_uv, w_out):
        heads = w_uk.shape[0]
        width = query.shape[1] // heads
        columns = w_out.shape[1] // tensor

        def body(*refs):
            kernel(seq, tensor, 1.0 / math.sqrt(width), *refs)

        smem = pl.BlockSpec(memory_space=pltpu.SMEM)
        vmem = pl.BlockSpec(memory_space=pltpu.VMEM)
        hbm = pl.BlockSpec(memory_space=pl.ANY)
        dma = pltpu.SemaphoreType.DMA
        return pl.pallas_call(
            body,
            out_shape=jax.ShapeDtypeStruct((query.shape[0], columns), jnp.bfloat16),
            in_specs=[smem, smem, vmem, hbm, hbm, hbm, hbm],
            out_specs=vmem,
            scratch_shapes=[
                pltpu.VMEM((seq, ROWS, LANES), jnp.bfloat16),
                pltpu.VMEM(cache.shape, cache.dtype),
                pltpu.VMEM(w_uk.shape, w_uk.dtype),
                pltpu.VMEM(w_uv.shape, w_uv.dtype),
                pltpu.VMEM(w_out.shape, w_out.dtype),
                pltpu.VMEM((page_owner.shape[0] * ROWS, LANES), jnp.float32),
                pltpu.VMEM((seq * ROWS, LANES), jnp.bfloat16),
                pltpu.VMEM((seq, ROWS, LANES), jnp.bfloat16),
                pltpu.VMEM((seq, ROWS, LANES), jnp.bfloat16),
                pltpu.VMEM((seq * ROWS, LANES), jnp.float32),
                pltpu.VMEM((tensor, 1, columns), jnp.float32),
                pltpu.VMEM((tensor, 1, columns), jnp.float32),
                dma((4,)),
                dma, dma, dma, dma,
                dma((tensor,)),
                dma((tensor,)),
            ],
            compiler_params=pltpu.CompilerParams(collective_id=0, has_side_effects=True),
        )(page_owner, page_fill, query, cache, w_uk, w_uv, w_out)

    return jax.shard_map(
        shards,
        mesh=mesh,
        in_specs=(
            P("seq", "tensor"), P("seq"), P("seq"), P("seq", None, None),
            P("tensor", None, None), P("tensor", None, None), P("tensor", None),
        ),
        out_specs=P("seq", "tensor"),
        check_vma=False,
    )
```

time: 1100 us -> 44 us (0.04)
  blocking collectives: 1040 us -> 0 us
  Pallas kernels: 0 us -> 42.6 us
  waiting for transfers between devices: 24.8 us -> 0 us
  between operations: 13.5 us -> 0.01 us
    unnamed x1 -> x0, blocking collectives: 491 us -> none
    pmax x1 -> x0, blocking collectives: 488 us -> none  [shards(): peak_score = lax.pmax(local_peak, 'seq')]
    all_gather x1 -> x0, blocking collectives: 58.9 us -> none  [shards(): gathered = lax.all_gather(query, 'seq', axis=0, tiled=True)]
    pallas_call x0 -> x1, Pallas kernels: none -> 42.6 us  [shards(): pl.pallas_call(body, out_shape=jax.ShapeDtypeStruct((query.shape[0], colu...]
    unnamed x4 -> x0, waiting for transfers between devices: 24.8 us -> none
  transfers between devices with their start and end apart: 2 -> 0, of which waited for: 1 -> 0; matrix products, arithmetic and copies ran while one was open for 0% -> 0% of each run, Pallas kernels for 0% -> 0%
where the time goes in v1:
time: 44 us; the launch traced here: 43.9 us
  Pallas kernels  42.6 us (97%)
  local copies, waits for them, and re-layouts  1.26 us (3%)
    pallas_call x1, Pallas kernels, shards(): pl.pallas_call(body, out_shape=jax.ShapeDtypeStruct((query.shape[0], colu...  42.6 us
    unnamed x1, local copies, waits for them, and re-layouts  1.26 us

profile of v1, /device:TPU:1, one launch (start us, length us, event | category | flops | bytes accessed | tf_op | source)
XLA Modules:
  0.0 43.9 jit_solution(12668038153215864537)
XLA Ops:
  0.0 42.6 %shard_map.73 = bf16[1,512]{1,0:T(2,128)(2,1)} custom-call(s32[16]{0:T(128)} %refs_0_.1, s32[16]{0:T(128)} %refs_1_.1, bf16[1,768]{1,0:T(2,128)(2,1)} %refs_2_.1, bf16[16,64,576]{2,1,0:T(8,128)(2,1)} %refs_3_.1, bf16[4,128,512]{2,1,0:T(8,128)(2,1)} %refs_4_.1, bf16[4,512,128]{2,1,0:T(8,128)(2,1)} %refs_5_.1, bf16[512,2048]{1,0:T(8,128)(2,1)} %refs_6_.1), custom_call_target="tpu_custom_call" | custom-call | tf_op jit(solution)/shard_map/pallas_call | solution.py:254
  42.6 1.3 %copy.9 = bf16[1,512]{1,0:T(2,128)(2,1)} copy(bf16[1,512]{1,0:T(2,128)(2,1)} %shard_map.73) | data formatting | bytes 2048

commit v2 on v1

v2 whole, which is shorter than its diff:
```python
import math

import jax
import jax.numpy as jnp
from jax import lax
from jax.experimental import pallas as pl
from jax.experimental.pallas import tpu as pltpu
from jax.sharding import PartitionSpec as P

MESH = pl.DeviceIdType.MESH
EMPTY = -1e30
LANES = 128
ROWS = 8
SENT = 6
NY = 8


def kernel(
    seq, tensor, scale, ny, nz,
    owner, fill, q_ref, cache_hbm, wuk_hbm, wuv_hbm, wout_hbm,
    out_ref,
    qmine, qearly, qlate, cache, wuk, wuv, wout, bias, sel, pick, sendb, recvb, rf, xs, xr,
    local_sems, send1, recv1, send2, recv2, bsend, brecv, xsend, xrecv,
):
    pages, page, width = cache.shape
    heads, nope, latent = wuk.shape
    rope = width - latent
    tokens = pages * page
    me = lax.axis_index("seq")
    tx = lax.axis_index("tensor")
    core = lax.rem(me, 2)
    y = lax.rem(lax.div(me, 2), ny)
    z = lax.div(me, 2 * ny)
    line = y * 2 + core
    deep = nz // 2
    late = lax.div(z, deep)
    slot = line * deep + lax.rem(z, deep)
    half = seq // 2

    def seat(z_at, line_at):
        return z_at * (2 * ny) + line_at

    def along_z(k):
        return seat(lax.rem(z + k, nz), line)

    def along_y(k):
        return seat(z, lax.rem(line + k, 2 * ny))

    barrier = pltpu.get_barrier_semaphore()
    for k in range(1, nz):
        pl.semaphore_signal(barrier, 1, device_id={"seq": along_z(k)}, device_id_type=MESH)
    for k in range(1, 2 * ny):
        pl.semaphore_signal(barrier, 1, device_id={"seq": along_y(k)}, device_id_type=MESH)
    for k in range(1, tensor):
        pl.semaphore_signal(
            barrier, 1, device_id={"tensor": lax.rem(tx + k, tensor)}, device_id_type=MESH
        )

    q = q_ref[...].astype(jnp.float32)
    step = nope + rope
    rows = [q[:, h * step : h * step + nope] for h in range(heads)]
    ropes = [q[:, h * step + nope : (h + 1) * step] for h in range(heads)]
    rows += [jnp.concatenate(ropes[h : h + 2], axis=1) for h in range(0, heads, 2)]
    rows += [jnp.zeros((ROWS - SENT, LANES), jnp.float32)]
    qmine[...] = jnp.concatenate(rows, axis=0).astype(jnp.bfloat16)[None]
    loads = [
        pltpu.make_async_copy(src, dst, local_sems.at[i])
        for i, (src, dst) in enumerate(
            ((wuk_hbm, wuk), (cache_hbm, cache), (wuv_hbm, wuv), (wout_hbm, wout))
        )
    ]
    queries = (qearly, qlate)
    sent = pl.ds(0, SENT)

    pl.semaphore_wait(barrier, nz - 1 + 2 * ny - 1 + tensor - 1)

    for part, buf in enumerate(queries):

        @pl.when(late == part)
        def _(part=part, buf=buf):
            for k in range(1, nz):
                pltpu.make_async_remote_copy(
                    src_ref=qmine.at[:, sent],
                    dst_ref=buf.at[pl.ds(slot, 1), sent],
                    send_sem=send1,
                    recv_sem=recv1.at[part],
                    device_id={"seq": along_z(k)},
                    device_id_type=MESH,
                ).start()
            pltpu.make_async_copy(
                qmine.at[:, sent], buf.at[pl.ds(slot, 1), sent], recv1.at[part]
            ).start()

    for load in loads:
        load.start()

    row16 = lax.broadcasted_iota(jnp.int32, (pages, LANES), 0)
    lane16 = lax.broadcasted_iota(jnp.int32, (pages, LANES), 1)
    own_row = jnp.zeros((pages, LANES), jnp.int32)
    own_lane = jnp.zeros((pages, LANES), jnp.int32)
    for p in range(pages):
        own_row = jnp.where(row16 == p, owner[p], own_row)
        own_lane = jnp.where((lane16 & (pages - 1)) == p, owner[p], own_lane)
    repeated = jnp.max(
        jnp.where((own_row == own_lane) & (row16 < (lane16 & (pages - 1))), 1, 0),
        axis=0, keepdims=True,
    )
    first_lane = jnp.where(repeated > 0, -1, own_lane[:1])
    big_row = lax.broadcasted_iota(jnp.int32, (seq * ROWS, LANES), 0)
    big_lane = lax.broadcasted_iota(jnp.int32, (seq * ROWS, LANES), 1)
    wanted = (first_lane * ROWS) + lax.div(big_lane[:1], pages)
    wanted = jnp.where((first_lane >= 0) & (big_lane[:1] < (heads + 1) * pages), wanted, -1)
    pick[...] = jnp.where(big_row == wanted, 1.0, 0.0).astype(jnp.bfloat16)
    own_rows = jnp.concatenate([own_row] * heads, axis=0)
    lane = lax.broadcasted_iota(jnp.int32, (1, LANES), 1)
    per = LANES // page
    for j in range(tokens // LANES):
        own_l = jnp.where(lane < page, owner[per * j], owner[per * j + 1])
        fill_l = jnp.where(lane < page, fill[per * j], fill[per * j + 1])
        own_l = jnp.where((lane & (page - 1)) < fill_l, own_l, -1)
        bias[:, j * LANES : (j + 1) * LANES] = jnp.where(own_rows == own_l, 0.0, EMPTY)

    for part, buf in enumerate(queries):
        whole = buf.at[pl.ds(0, deep), sent]
        pltpu.make_async_copy(whole, whole, recv1.at[part]).wait()
        mine = buf.at[pl.ds(line * deep, deep), sent]
        for k in range(1, 2 * ny):
            pltpu.make_async_remote_copy(
                src_ref=mine,
                dst_ref=mine,
                send_sem=send2,
                recv_sem=recv2.at[part],
                device_id={"seq": along_y(k)},
                device_id_type=MESH,
            ).start()

    for part, buf in enumerate(queries):
        rest = buf.at[pl.ds(0, (2 * ny - 1) * deep), sent]
        pltpu.make_async_copy(rest, rest, recv2.at[part]).wait()
        for p in range(pages):
            at = (owner[p] & (2 * ny - 1)) * deep + ((owner[p] // (2 * ny)) & (deep - 1))
            sel[p * ROWS : (p + 1) * ROWS, :] = buf[at].astype(jnp.float32)
        if part == 0:
            loads[0].wait()
        joined = []
        for h in range(heads):
            plain = sel[pl.ds(h, pages, stride=ROWS), :].astype(jnp.bfloat16)
            pair = sel[pl.ds(heads + h // 2, pages, stride=ROWS), :]
            turned = pair[:, (h % 2) * rope : (h % 2 + 1) * rope].astype(jnp.bfloat16)
            lat = jnp.dot(plain, wuk[h], preferred_element_type=jnp.float32)
            joined.append(jnp.concatenate([lat.astype(jnp.bfloat16), turned], axis=1))
        joined = jnp.concatenate(joined, axis=0)

        if part == 0:
            loads[1].wait()
        keys = cache[...].reshape(tokens, width)
        scores = lax.dot_general(
            joined, keys, (((1,), (1,)), ((), ())), preferred_element_type=jnp.float32
        )
        scores = scores * scale + bias[...]
        top = jnp.max(scores, axis=1, keepdims=True)
        top = jnp.where(top > 0.5 * EMPTY, top, 0.0)
        top_hi = top.astype(jnp.bfloat16).astype(jnp.float32)
        top_lo = (top - top_hi).astype(jnp.bfloat16).astype(jnp.float32)
        weights = jnp.exp(scores - (top_hi + top_lo))
        total = jnp.sum(weights, axis=1, keepdims=True)
        total_hi = total.astype(jnp.bfloat16).astype(jnp.float32)
        total_lo = total - total_hi
        sums = jnp.dot(
            weights.astype(jnp.bfloat16), keys[:, :latent], preferred_element_type=jnp.float32
        )

        if part == 0:
            loads[2].wait()
        blocks = [
            jnp.dot(
                sums[h * pages : (h + 1) * pages].astype(jnp.bfloat16), wuv[h],
                preferred_element_type=jnp.float32,
            )
            for h in range(heads)
        ]
        stats = jnp.zeros((pages, LANES), jnp.float32)
        for i, piece in enumerate((top_hi, top_lo, total_hi, total_lo)):
            for h in range(heads):
                stats = jnp.where(
                    lane16 == i * heads + h, piece[h * pages : (h + 1) * pages], stats
                )
        blocks += [stats, jnp.zeros((LANES - (heads + 1) * pages, LANES), jnp.float32)]
        table = jnp.concatenate(blocks, axis=0).astype(jnp.bfloat16)
        sendb[pl.ds(part * half, half)] = (
            jnp.dot(
                pick[pl.ds(part * half * ROWS, half * ROWS), :], table,
                preferred_element_type=jnp.float32,
            )
            .astype(jnp.bfloat16)
            .reshape(half, ROWS, LANES)
        )

        def send_sums(k, c, part=part):
            peer = part * half + lax.rem(me + k, half)
            pltpu.make_async_remote_copy(
                src_ref=sendb.at[peer, sent],
                dst_ref=recvb.at[me, sent],
                send_sem=bsend,
                recv_sem=brecv,
                device_id={"seq": peer},
                device_id_type=MESH,
            ).start()
            return c

        lax.fori_loop(jnp.where(late == part, 1, 0), half, send_sums, 0)

    recvb[me] = sendb[me]
    others = recvb.at[pl.ds(0, seq - 1), sent]
    pltpu.make_async_copy(others, others, brecv).wait()

    rf[...] = recvb[...].reshape(seq * ROWS, LANES).astype(jnp.float32)
    got = rf[pl.ds(heads, seq, stride=ROWS), :]
    tops = got + pltpu.roll(got, LANES - heads, 1)
    totals = pltpu.roll(got, LANES - 2 * heads, 1) + pltpu.roll(got, LANES - 3 * heads, 1)
    some = totals > 0.0
    tops = jnp.where(some, tops, EMPTY)
    peak = jnp.max(tops, axis=0, keepdims=True)
    share = jnp.where(some, jnp.exp(tops - peak), 0.0)
    denominator = jnp.sum(jnp.where(some, share * totals, 0.0), axis=0, keepdims=True)
    outs = []
    for h in range(heads):
        mine = rf[pl.ds(h, seq, stride=ROWS), :]
        numerator = jnp.sum(mine * share[:, h : h + 1], axis=0, keepdims=True)
        outs.append(numerator / denominator[:, h : h + 1])
    head_out = jnp.concatenate(outs, axis=1).astype(jnp.bfloat16)

    loads[3].wait()
    partial_value = jnp.dot(head_out, wout[...], preferred_element_type=jnp.float32)
    columns = partial_value.shape[1] // tensor
    for t in range(tensor):
        xs[t] = partial_value[:, t * columns : (t + 1) * columns]
    xr[tx] = xs[tx]
    sends = []
    for k in range(1, tensor):
        peer = lax.rem(tx + k, tensor)
        sends.append(
            pltpu.make_async_remote_copy(
                src_ref=xs.at[peer],
                dst_ref=xr.at[tx],
                send_sem=xsend.at[k],
                recv_sem=xrecv.at[k],
                device_id={"tensor": peer},
                device_id_type=MESH,
            )
        )
    for send in sends:
        send.start()
    for send in sends:
        send.wait_recv()
    total_value = xr[0]
    for t in range(1, tensor):
        total_value = total_value + xr[t]
    out_ref[...] = total_value.astype(out_ref.dtype)
    for send in sends:
        send.wait_send()
    away = qearly.at[pl.ds(0, nz - 1), sent]
    pltpu.make_async_copy(away, away, send1).wait()
    for buf in queries:
        away = buf.at[pl.ds(0, (2 * ny - 1) * deep), sent]
        pltpu.make_async_copy(away, away, send2).wait()
    away = sendb.at[pl.ds(0, seq - 1), sent]
    pltpu.make_async_copy(away, away, bsend).wait()


def solution(mesh):
    seq, tensor = mesh.shape["seq"], mesh.shape["tensor"]

    def shards(query, page_owner, page_fill, cache, w_uk, w_uv, w_out):
        heads = w_uk.shape[0]
        width = query.shape[1] // heads
        columns = w_out.shape[1] // tensor
        ny = NY

        def body(*refs):
            kernel(seq, tensor, 1.0 / math.sqrt(width), ny, seq // (2 * ny), *refs)

        smem = pl.BlockSpec(memory_space=pltpu.SMEM)
        vmem = pl.BlockSpec(memory_space=pltpu.VMEM)
        hbm = pl.BlockSpec(memory_space=pl.ANY)
        dma = pltpu.SemaphoreType.DMA
        return pl.pallas_call(
            body,
            out_shape=jax.ShapeDtypeStruct((query.shape[0], columns), jnp.bfloat16),
            in_specs=[smem, smem, vmem, hbm, hbm, hbm, hbm],
            out_specs=vmem,
            scratch_shapes=[
                pltpu.VMEM((1, ROWS, LANES), jnp.bfloat16),
                pltpu.VMEM((seq // 2, ROWS, LANES), jnp.bfloat16),
                pltpu.VMEM((seq // 2, ROWS, LANES), jnp.bfloat16),
                pltpu.VMEM(cache.shape, cache.dtype),
                pltpu.VMEM(w_uk.shape, w_uk.dtype),
                pltpu.VMEM(w_uv.shape, w_uv.dtype),
                pltpu.VMEM(w_out.shape, w_out.dtype),
                pltpu.VMEM((page_owner.shape[0] * heads, cache.shape[0] * cache.shape[1]), jnp.float32),
                pltpu.VMEM((page_owner.shape[0] * ROWS, LANES), jnp.float32),
                pltpu.VMEM((seq * ROWS, LANES), jnp.bfloat16),
                pltpu.VMEM((seq, ROWS, LANES), jnp.bfloat16),
                pltpu.VMEM((seq, ROWS, LANES), jnp.bfloat16),
                pltpu.VMEM((seq * ROWS, LANES), jnp.float32),
                pltpu.VMEM((tensor, 1, columns), jnp.float32),
                pltpu.VMEM((tensor, 1, columns), jnp.float32),
                dma((4,)),
                dma,
                dma((2,)),
                dma,
                dma((2,)),
                dma, dma,
                dma((tensor,)),
                dma((tensor,)),
            ],
            compiler_params=pltpu.CompilerParams(collective_id=0, has_side_effects=True),
        )(page_owner, page_fill, query, cache, w_uk, w_uv, w_out)

    return jax.shard_map(
        shards,
        mesh=mesh,
        in_specs=(
            P("seq", "tensor"), P("seq"), P("seq"), P("seq", None, None),
            P("tensor", None, None), P("tensor", None, None), P("tensor", None),
        ),
        out_specs=P("seq", "tensor"),
        check_vma=False,
    )
```

time: 44 us -> 41.5 us (0.943)
  Pallas kernels: 42.6 us -> 40.1 us
    pallas_call x1, Pallas kernels: 42.6 us -> 40.1 us  [shards(): pl.pallas_call(body, out_shape=jax.ShapeDtypeStruct((query.shape[0], colu...]
where the time goes in v2:
time: 41.5 us; the launch traced here: 41.4 us
  Pallas kernels  40.1 us (97%)
  local copies, waits for them, and re-layouts  1.26 us (3%)
    pallas_call x1, Pallas kernels, shards(): pl.pallas_call(body, out_shape=jax.ShapeDtypeStruct((query.shape[0], colu...  40.1 us
    unnamed x1, local copies, waits for them, and re-layouts  1.26 us

profile of v2, /device:TPU:1, one launch (start us, length us, event | category | flops | bytes accessed | tf_op | source)
XLA Modules:
  0.0 41.4 jit_solution(12469695678585392429)
XLA Ops:
  0.0 40.1 %shard_map.73 = bf16[1,512]{1,0:T(2,128)(2,1)} custom-call(s32[16]{0:T(128)} %refs_0_.1, s32[16]{0:T(128)} %refs_1_.1, bf16[1,768]{1,0:T(2,128)(2,1)} %refs_2_.1, bf16[16,64,576]{2,1,0:T(8,128)(2,1)} %refs_3_.1, bf16[4,128,512]{2,1,0:T(8,128)(2,1)} %refs_4_.1, bf16[4,512,128]{2,1,0:T(8,128)(2,1)} %refs_5_.1, bf16[512,2048]{1,0:T(8,128)(2,1)} %refs_6_.1), custom_call_target="tpu_custom_call" | custom-call | tf_op jit(solution)/shard_map/pallas_call | solution.py:287
  40.1 1.3 %copy.9 = bf16[1,512]{1,0:T(2,128)(2,1)} copy(bf16[1,512]{1,0:T(2,128)(2,1)} %shard_map.73) | data formatting | bytes 2048

commit v3 on v2

--- a/solution.py
+++ b/solution.py
@@ -1,3 +1,4 @@
+import functools
 import math
 
 import jax
@@ -17,15 +18,16 @@
 
 def kernel(
     seq, tensor, scale, ny, nz,
-    owner, fill, q_ref, cache_hbm, wuk_hbm, wuv_hbm, wout_hbm,
+    owner_hbm, fill_hbm, q_hbm, cache_hbm, wuk_hbm, wuv_hbm, wout_hbm,
     out_ref,
-    qmine, qearly, qlate, cache, wuk, wuv, wout, bias, sel, pick, sendb, recvb, rf, xs, xr,
+    owner, fill, q_ref, qmine, qearly, qlate, cache, wuk, wuv, wout, bias, sel, pick, sendb, recvb, rf, xs, xr,
     local_sems, send1, recv1, send2, recv2, bsend, brecv, xsend, xrecv,
 ):
     pages, page, width = cache.shape
     heads, nope, latent = wuk.shape
     rope = width - latent
     tokens = pages * page
+    columns = wout.shape[2]
     me = lax.axis_index("seq")
     tx = lax.axis_index("tensor")
     core = lax.rem(me, 2)
@@ -46,6 +48,12 @@
     def along_y(k):
         return seat(z, lax.rem(line + k, 2 * ny))
 
+    small = [
+        pltpu.make_async_copy(src, dst, local_sems.at[i])
+        for i, (src, dst) in enumerate(((q_hbm, q_ref), (owner_hbm, owner), (fill_hbm, fill)))
+    ]
+    small[0].start()
+
     barrier = pltpu.get_barrier_semaphore()
     for k in range(1, nz):
         pl.semaphore_signal(barrier, 1, device_id={"seq": along_z(k)}, device_id_type=MESH)
@@ -56,6 +64,10 @@
             barrier, 1, device_id={"tensor": lax.rem(tx + k, tensor)}, device_id_type=MESH
         )
 
+    small[1].start()
+    small[2].start()
+
+    small[0].wait()
     q = q_ref[...].astype(jnp.float32)
     step = nope + rope
     rows = [q[:, h * step : h * step + nope] for h in range(heads)]
@@ -64,9 +76,10 @@
     rows += [jnp.zeros((ROWS - SENT, LANES), jnp.float32)]
     qmine[...] = jnp.concatenate(rows, axis=0).astype(jnp.bfloat16)[None]
     loads = [
-        pltpu.make_async_copy(src, dst, local_sems.at[i])
+        pltpu.make_async_copy(src, dst, local_sems.at[3 + i])
         for i, (src, dst) in enumerate(
-            ((wuk_hbm, wuk), (cache_hbm, cache), (wuv_hbm, wuv), (wout_hbm, wout))
+            ((wuk_hbm, wuk), (cache_hbm, cache), (wuv_hbm, wuv))
+            + tuple((wout_hbm.at[:, pl.ds(t * columns, columns)], wout.at[t]) for t in range(tensor))
         )
     ]
     queries = (qearly, qlate)
@@ -94,6 +107,8 @@
     for load in loads:
         load.start()
 
+    small[1].wait()
+    small[2].wait()
     row16 = lax.broadcasted_iota(jnp.int32, (pages, LANES), 0)
     lane16 = lax.broadcasted_iota(jnp.int32, (pages, LANES), 1)
     own_row = jnp.zeros((pages, LANES), jnp.int32)
@@ -196,8 +211,8 @@
             .reshape(half, ROWS, LANES)
         )
 
-        def send_sums(k, c, part=part):
-            peer = part * half + lax.rem(me + k, half)
+        def send_sums(k, c, base):
+            peer = base + lax.rem(line + k, 2 * ny)
             pltpu.make_async_remote_copy(
                 src_ref=sendb.at[peer, sent],
                 dst_ref=recvb.at[me, sent],
@@ -208,7 +223,11 @@
             ).start()
             return c
 
-        lax.fori_loop(jnp.where(late == part, 1, 0), half, send_sums, 0)
+        for level in range(part * deep, (part + 1) * deep):
+            lax.fori_loop(
+                jnp.where(z == level, 1, 0), 2 * ny,
+                functools.partial(send_sums, base=level * 2 * ny), 0,
+            )
 
     recvb[me] = sendb[me]
     others = recvb.at[pl.ds(0, seq - 1), sent]
@@ -230,15 +249,16 @@
         outs.append(numerator / denominator[:, h : h + 1])
     head_out = jnp.concatenate(outs, axis=1).astype(jnp.bfloat16)
 
-    loads[3].wait()
-    partial_value = jnp.dot(head_out, wout[...], preferred_element_type=jnp.float32)
-    columns = partial_value.shape[1] // tensor
-    for t in range(tensor):
-        xs[t] = partial_value[:, t * columns : (t + 1) * columns]
-    xr[tx] = xs[tx]
+    for load in loads[3:]:
+        load.wait()
     sends = []
-    for k in range(1, tensor):
+    for k in [2, 1, 3, 0]:
         peer = lax.rem(tx + k, tensor)
+        piece = jnp.dot(head_out, wout[peer], preferred_element_type=jnp.float32)
+        if k == 0:
+            xr[tx] = piece
+            continue
+        xs[peer] = piece
         sends.append(
             pltpu.make_async_remote_copy(
                 src_ref=xs.at[peer],
@@ -249,8 +269,7 @@
                 device_id_type=MESH,
             )
         )
-    for send in sends:
-        send.start()
+        sends[-1].start()
     for send in sends:
         send.wait_recv()
     total_value = xr[0]
@@ -280,23 +299,25 @@
         def body(*refs):
             kernel(seq, tensor, 1.0 / math.sqrt(width), ny, seq // (2 * ny), *refs)
 
-        smem = pl.BlockSpec(memory_space=pltpu.SMEM)
         vmem = pl.BlockSpec(memory_space=pltpu.VMEM)
-        hbm = pl.BlockSpec(memory_space=pl.ANY)
+        hbm = pl.BlockSpec(memory_space=pltpu.HBM)
         dma = pltpu.SemaphoreType.DMA
         return pl.pallas_call(
             body,
-            out_shape=jax.ShapeDtypeStruct((query.shape[0], columns), jnp.bfloat16),
-            in_specs=[smem, smem, vmem, hbm, hbm, hbm, hbm],
+            out_shape=pltpu.VMEM((query.shape[0], columns), jnp.bfloat16),
+            in_specs=[hbm] * 7,
             out_specs=vmem,
             scratch_shapes=[
+                pltpu.SMEM(page_owner.shape, page_owner.dtype),
+                pltpu.SMEM(page_fill.shape, page_fill.dtype),
+                pltpu.VMEM(query.shape, query.dtype),
                 pltpu.VMEM((1, ROWS, LANES), jnp.bfloat16),
                 pltpu.VMEM((seq // 2, ROWS, LANES), jnp.bfloat16),
                 pltpu.VMEM((seq // 2, ROWS, LANES), jnp.bfloat16),
                 pltpu.VMEM(cache.shape, cache.dtype),
                 pltpu.VMEM(w_uk.shape, w_uk.dtype),
                 pltpu.VMEM(w_uv.shape, w_uv.dtype),
-                pltpu.VMEM(w_out.shape, w_out.dtype),
+                pltpu.VMEM((tensor, w_out.shape[0], columns), w_out.dtype),
                 pltpu.VMEM((page_owner.shape[0] * heads, cache.shape[0] * cache.shape[1]), jnp.float32),
                 pltpu.VMEM((page_owner.shape[0] * ROWS, LANES), jnp.float32),
                 pltpu.VMEM((seq * ROWS, LANES), jnp.bfloat16),
@@ -305,7 +326,7 @@
                 pltpu.VMEM((seq * ROWS, LANES), jnp.float32),
                 pltpu.VMEM((tensor, 1, columns), jnp.float32),
                 pltpu.VMEM((tensor, 1, columns), jnp.float32),
-                dma((4,)),
+                dma((10,)),
                 dma,
                 dma((2,)),
                 dma,

time: 41.5 us -> 38 us (0.916)
  Pallas kernels: 40.1 us -> 37.3 us
  local copies, waits for them, and re-layouts: 1.26 us -> 0.58 us
    pallas_call x1, Pallas kernels: 40.1 us -> 37.3 us  [shards(): pl.pallas_call(body, out_shape=pltpu.VMEM((query.shape[0], columns), jnp....]
    unnamed x1, local copies, waits for them, and re-layouts: 1.26 us -> 0.58 us
where the time goes in v3:
time: 38 us; the launch traced here: 37.9 us
  Pallas kernels  37.3 us (98%)
  local copies, waits for them, and re-layouts  0.58 us (2%)
    pallas_call x1, Pallas kernels, shards(): pl.pallas_call(body, out_shape=pltpu.VMEM((query.shape[0], columns), jnp....  37.3 us

profile of v3, /device:TPU:1, one launch (start us, length us, event | category | flops | bytes accessed | tf_op | source)
XLA Modules:
  0.0 37.9 jit_solution(9762870143455961858)
XLA Ops:
  0.0 37.3 %shard_map.73 = bf16[1,512]{1,0:T(2,128)(2,1)S(1)} custom-call(s32[16]{0:T(128)} %refs_0_.1, s32[16]{0:T(128)} %refs_1_.1, bf16[1,768]{1,0:T(2,128)(2,1)} %refs_2_.1, bf16[16,64,576]{2,1,0:T(8,128)(2,1)} %refs_3_.1, bf16[4,128,512]{2,1,0:T(8,128)(2,1)} %refs_4_.1, bf16[4,512,128]{2,1,0:T(8,128)(2,1)} %refs_5_.1, bf16[512,2048]{1,0:T(8,128)(2,1)} %refs_6_.1), custom_call_target="tpu_custom_call" | custom-call | tf_op jit(solution)/shard_map/pallas_call | solution.py:305
  37.3 0.6 %copy.9 = bf16[1,512]{1,0:T(2,128)(2,1)} copy(bf16[1,512]{1,0:T(2,128)(2,1)S(1)} %shard_map.73) | data formatting | bytes 2048

commit v4 on v3

--- a/solution.py
+++ b/solution.py
@@ -21,7 +21,7 @@
     owner_hbm, fill_hbm, q_hbm, cache_hbm, wuk_hbm, wuv_hbm, wout_hbm,
     out_ref,
     owner, fill, q_ref, qmine, qearly, qlate, cache, wuk, wuv, wout, bias, sel, pick, sendb, recvb, rf, xs, xr,
-    local_sems, send1, recv1, send2, recv2, bsend, brecv, xsend, xrecv,
+    joined_sem, local_sems, send1, recv1, send2, recv2, bsend, brecv, xsend, xrecv,
 ):
     pages, page, width = cache.shape
     heads, nope, latent = wuk.shape
@@ -33,20 +33,18 @@
     core = lax.rem(me, 2)
     y = lax.rem(lax.div(me, 2), ny)
     z = lax.div(me, 2 * ny)
-    line = y * 2 + core
     deep = nz // 2
     late = lax.div(z, deep)
-    slot = line * deep + lax.rem(z, deep)
+    line = z * 2 + core
+    block = lax.rem(line, 2 * deep) * ny
     half = seq // 2
 
-    def seat(z_at, line_at):
-        return z_at * (2 * ny) + line_at
-
-    def along_z(k):
-        return seat(lax.rem(z + k, nz), line)
-
     def along_y(k):
-        return seat(z, lax.rem(line + k, 2 * ny))
+        return (z * ny + lax.rem(y + k, ny)) * 2 + core
+
+    def in_half(part, k):
+        at = part * 2 * deep + lax.rem(line + k, 2 * deep)
+        return (lax.div(at, 2) * ny + y) * 2 + lax.rem(at, 2)
 
     small = [
         pltpu.make_async_copy(src, dst, local_sems.at[i])
@@ -55,10 +53,24 @@
     small[0].start()
 
     barrier = pltpu.get_barrier_semaphore()
-    for k in range(1, nz):
-        pl.semaphore_signal(barrier, 1, device_id={"seq": along_z(k)}, device_id_type=MESH)
-    for k in range(1, 2 * ny):
-        pl.semaphore_signal(barrier, 1, device_id={"seq": along_y(k)}, device_id_type=MESH)
+    def tell(sem, peer):
+        pl.semaphore_signal(sem, 1, device_id={"seq": peer}, device_id_type=MESH)
+
+    def tell_half(sem, part, others_only):
+        for k in range(2 * deep):
+            peer = in_half(part, k)
+            if others_only and k == 0:
+                continue
+            tell(sem, peer)
+
+    for k in range(1, ny):
+        tell(barrier, along_y(k))
+
+    @pl.when(late == 0)
+    def _():
+        tell_half(barrier, 0, True)
+        tell_half(barrier, 1, False)
+
     for k in range(1, tensor):
         pl.semaphore_signal(
             barrier, 1, device_id={"tensor": lax.rem(tx + k, tensor)}, device_id_type=MESH
@@ -85,24 +97,31 @@
     queries = (qearly, qlate)
     sent = pl.ds(0, SENT)
 
-    pl.semaphore_wait(barrier, nz - 1 + 2 * ny - 1 + tensor - 1)
+    @pl.when(late == 0)
+    def _():
+        pl.semaphore_wait(barrier, ny - 1 + 2 * deep - 1 + tensor - 1)
+
+    @pl.when(late == 1)
+    def _():
+        pl.semaphore_wait(barrier, ny - 1 + 2 * deep + tensor - 1)
+        tell_half(joined_sem, 0, False)
+
 
     for part, buf in enumerate(queries):
 
         @pl.when(late == part)
-        def _(part=part, buf=buf):
-            for k in range(1, nz):
+        def _(buf=buf):
+            mine = buf.at[pl.ds(block + y, 1), sent]
+            for k in range(1, ny):
                 pltpu.make_async_remote_copy(
                     src_ref=qmine.at[:, sent],
-                    dst_ref=buf.at[pl.ds(slot, 1), sent],
+                    dst_ref=mine,
                     send_sem=send1,
-                    recv_sem=recv1.at[part],
-                    device_id={"seq": along_z(k)},
+                    recv_sem=recv1,
+                    device_id={"seq": along_y(k)},
                     device_id_type=MESH,
                 ).start()
-            pltpu.make_async_copy(
-                qmine.at[:, sent], buf.at[pl.ds(slot, 1), sent], recv1.at[part]
-            ).start()
+            pltpu.make_async_copy(qmine.at[:, sent], mine, recv1).start()
 
     for load in loads:
         load.start()
@@ -135,25 +154,41 @@
         own_l = jnp.where((lane & (page - 1)) < fill_l, own_l, -1)
         bias[:, j * LANES : (j + 1) * LANES] = jnp.where(own_rows == own_l, 0.0, EMPTY)
 
-    for part, buf in enumerate(queries):
-        whole = buf.at[pl.ds(0, deep), sent]
-        pltpu.make_async_copy(whole, whole, recv1.at[part]).wait()
-        mine = buf.at[pl.ds(line * deep, deep), sent]
-        for k in range(1, 2 * ny):
+    def send_line(part, to):
+        mine = queries[part].at[pl.ds(block, ny), sent]
+        for k in range(1 if part == to else 0, 2 * deep):
             pltpu.make_async_remote_copy(
                 src_ref=mine,
                 dst_ref=mine,
                 send_sem=send2,
                 recv_sem=recv2.at[part],
-                device_id={"seq": along_y(k)},
+                device_id={"seq": in_half(to, k)},
                 device_id_type=MESH,
             ).start()
 
     for part, buf in enumerate(queries):
-        rest = buf.at[pl.ds(0, (2 * ny - 1) * deep), sent]
-        pltpu.make_async_copy(rest, rest, recv2.at[part]).wait()
+
+        @pl.when(late == part)
+        def _(part=part, buf=buf):
+            mine = buf.at[pl.ds(block, ny), sent]
+            pltpu.make_async_copy(mine, mine, recv1).wait()
+            send_line(part, 0)
+            pl.semaphore_wait(joined_sem, 2 * deep)
+            send_line(part, 1)
+            if part == 0:
+                tell_half(joined_sem, 1, False)
+
+    for part, buf in enumerate(queries):
+        for own, lines in ((part, 2 * deep - 1), (1 - part, 2 * deep)):
+
+            @pl.when(late == own)
+            def _(part=part, buf=buf, lines=lines):
+                rest = buf.at[pl.ds(0, lines * ny), sent]
+                pltpu.make_async_copy(rest, rest, recv2.at[part]).wait()
+
         for p in range(pages):
-            at = (owner[p] & (2 * ny - 1)) * deep + ((owner[p] // (2 * ny)) & (deep - 1))
+            spot = owner[p] & (half - 1)
+            at = ((spot // (2 * ny)) * 2 + (spot & 1)) * ny + ((spot // 2) & (ny - 1))
             sel[p * ROWS : (p + 1) * ROWS, :] = buf[at].astype(jnp.float32)
         if part == 0:
             loads[0].wait()
@@ -212,7 +247,7 @@
         )
 
         def send_sums(k, c, base):
-            peer = base + lax.rem(line + k, 2 * ny)
+            peer = base + lax.rem(me + k, 2 * ny)
             pltpu.make_async_remote_copy(
                 src_ref=sendb.at[peer, sent],
                 dst_ref=recvb.at[me, sent],
@@ -278,10 +313,10 @@
     out_ref[...] = total_value.astype(out_ref.dtype)
     for send in sends:
         send.wait_send()
-    away = qearly.at[pl.ds(0, nz - 1), sent]
+    away = qearly.at[pl.ds(0, ny - 1), sent]
     pltpu.make_async_copy(away, away, send1).wait()
-    for buf in queries:
-        away = buf.at[pl.ds(0, (2 * ny - 1) * deep), sent]
+    for _ in range(2 * nz - 1):
+        away = qearly.at[pl.ds(0, ny), sent]
         pltpu.make_async_copy(away, away, send2).wait()
     away = sendb.at[pl.ds(0, seq - 1), sent]
     pltpu.make_async_copy(away, away, bsend).wait()
@@ -326,10 +361,9 @@
                 pltpu.VMEM((seq * ROWS, LANES), jnp.float32),
                 pltpu.VMEM((tensor, 1, columns), jnp.float32),
                 pltpu.VMEM((tensor, 1, columns), jnp.float32),
+                pltpu.SemaphoreType.REGULAR,
                 dma((10,)),
-                dma,
-                dma((2,)),
-                dma,
+                dma, dma, dma,
                 dma((2,)),
                 dma, dma,
                 dma((tensor,)),

time: 38 us -> 37 us (0.974)
  Pallas kernels: 37.3 us -> 36.3 us
    pallas_call x1, Pallas kernels: 37.3 us -> 36.3 us  [shards(): pl.pallas_call(body, out_shape=pltpu.VMEM((query.shape[0], columns), jnp....]
where the time goes in v4:
time: 37 us; the launch traced here: 36.9 us
  Pallas kernels  36.3 us (98%)
  local copies, waits for them, and re-layouts  0.58 us (2%)
    pallas_call x1, Pallas kernels, shards(): pl.pallas_call(body, out_shape=pltpu.VMEM((query.shape[0], columns), jnp....  36.3 us

profile of v4, /device:TPU:1, one launch (start us, length us, event | category | flops | bytes accessed | tf_op | source)
XLA Modules:
  0.0 36.9 jit_solution(14464355008932087547)
XLA Ops:
  0.0 36.3 %shard_map.73 = bf16[1,512]{1,0:T(2,128)(2,1)S(1)} custom-call(s32[16]{0:T(128)} %refs_0_.1, s32[16]{0:T(128)} %refs_1_.1, bf16[1,768]{1,0:T(2,128)(2,1)} %refs_2_.1, bf16[16,64,576]{2,1,0:T(8,128)(2,1)} %refs_3_.1, bf16[4,128,512]{2,1,0:T(8,128)(2,1)} %refs_4_.1, bf16[4,512,128]{2,1,0:T(8,128)(2,1)} %refs_5_.1, bf16[512,2048]{1,0:T(8,128)(2,1)} %refs_6_.1), custom_call_target="tpu_custom_call" | custom-call | tf_op jit(solution)/shard_map/pallas_call | solution.py:340
  36.3 0.6 %copy.9 = bf16[1,512]{1,0:T(2,128)(2,1)} copy(bf16[1,512]{1,0:T(2,128)(2,1)S(1)} %shard_map.73) | data formatting | bytes 2048

commit v5 on v4

--- a/solution.py
+++ b/solution.py
@@ -21,7 +21,7 @@
     owner_hbm, fill_hbm, q_hbm, cache_hbm, wuk_hbm, wuv_hbm, wout_hbm,
     out_ref,
     owner, fill, q_ref, qmine, qearly, qlate, cache, wuk, wuv, wout, bias, sel, pick, sendb, recvb, rf, xs, xr,
-    joined_sem, local_sems, send1, recv1, send2, recv2, bsend, brecv, xsend, xrecv,
+    chip_in, line_in, local_sems, send1, recv1, send2, recv2, bsend, brecv, xsend, xrecv,
 ):
     pages, page, width = cache.shape
     heads, nope, latent = wuk.shape
@@ -53,6 +53,7 @@
     small[0].start()
 
     barrier = pltpu.get_barrier_semaphore()
+
     def tell(sem, peer):
         pl.semaphore_signal(sem, 1, device_id={"seq": peer}, device_id_type=MESH)
 
@@ -63,21 +64,41 @@
                 continue
             tell(sem, peer)
 
-    for k in range(1, ny):
-        tell(barrier, along_y(k))
+    def tell_tensor(seat):
+        for k in range(1, tensor):
+            pl.semaphore_signal(
+                barrier, 1,
+                device_id={"seq": seat, "tensor": lax.rem(tx + k, tensor)},
+                device_id_type=MESH,
+            )
+
+    first_core, sibling = me - core, me + 1 - 2 * core
 
     @pl.when(late == 0)
     def _():
+        for k in range(1, ny):
+            tell(barrier, along_y(k))
         tell_half(barrier, 0, True)
-        tell_half(barrier, 1, False)
-
-    for k in range(1, tensor):
-        pl.semaphore_signal(
-            barrier, 1, device_id={"tensor": lax.rem(tx + k, tensor)}, device_id_type=MESH
-        )
+        for k in range(deep):
+            tell(barrier, (deep + lax.rem(z + k, deep)) * 2 * ny + y * 2)
+        tell_tensor(me)
+
+    @pl.when(late == 1)
+    def _():
+        tell(barrier, sibling)
+        for k in range(1, ny):
+            tell(barrier, along_y(k) + 1 - core)
+        tell_tensor(first_core + 1)
 
     small[1].start()
     small[2].start()
+
+    @pl.when((late == 1) & (core == 0))
+    def _():
+        pl.semaphore_wait(barrier, 2 * deep + 1)
+        for k in range(2 * deep):
+            tell(chip_in.at[z - deep], in_half(0, k))
+        tell(line_in.at[0], sibling)
 
     small[0].wait()
     q = q_ref[...].astype(jnp.float32)
@@ -101,11 +122,14 @@
     def _():
         pl.semaphore_wait(barrier, ny - 1 + 2 * deep - 1 + tensor - 1)
 
+    @pl.when((late == 1) & (core == 1))
+    def _():
+        pl.semaphore_wait(barrier, 2 * (ny - 1) + 2 * (tensor - 1) + 1)
+        tell(line_in.at[0], sibling)
+
     @pl.when(late == 1)
     def _():
-        pl.semaphore_wait(barrier, ny - 1 + 2 * deep + tensor - 1)
-        tell_half(joined_sem, 0, False)
-
+        pl.semaphore_wait(line_in.at[0], 1)
 
     for part, buf in enumerate(queries):
 
@@ -154,15 +178,15 @@
         own_l = jnp.where((lane & (page - 1)) < fill_l, own_l, -1)
         bias[:, j * LANES : (j + 1) * LANES] = jnp.where(own_rows == own_l, 0.0, EMPTY)
 
-    def send_line(part, to):
+    def send_line(part, peers):
         mine = queries[part].at[pl.ds(block, ny), sent]
-        for k in range(1 if part == to else 0, 2 * deep):
+        for peer in peers:
             pltpu.make_async_remote_copy(
                 src_ref=mine,
                 dst_ref=mine,
                 send_sem=send2,
                 recv_sem=recv2.at[part],
-                device_id={"seq": in_half(to, k)},
+                device_id={"seq": peer},
                 device_id_type=MESH,
             ).start()
 
@@ -172,11 +196,17 @@
         def _(part=part, buf=buf):
             mine = buf.at[pl.ds(block, ny), sent]
             pltpu.make_async_copy(mine, mine, recv1).wait()
-            send_line(part, 0)
-            pl.semaphore_wait(joined_sem, 2 * deep)
-            send_line(part, 1)
             if part == 0:
-                tell_half(joined_sem, 1, False)
+                send_line(0, [in_half(0, k) for k in range(1, 2 * deep)])
+                for j in range(deep):
+                    pl.semaphore_wait(chip_in.at[j], 1)
+                    send_line(0, [((deep + j) * ny + y) * 2 + c for c in range(2)])
+                for k in range(2 * deep):
+                    tell(line_in.at[1], in_half(1, k))
+            else:
+                send_line(1, [in_half(0, k) for k in range(2 * deep)])
+                pl.semaphore_wait(line_in.at[1], 2 * deep)
+                send_line(1, [in_half(1, k) for k in range(1, 2 * deep)])
 
     for part, buf in enumerate(queries):
         for own, lines in ((part, 2 * deep - 1), (1 - part, 2 * deep)):
@@ -361,7 +391,8 @@
                 pltpu.VMEM((seq * ROWS, LANES), jnp.float32),
                 pltpu.VMEM((tensor, 1, columns), jnp.float32),
                 pltpu.VMEM((tensor, 1, columns), jnp.float32),
-                pltpu.SemaphoreType.REGULAR,
+                pltpu.SemaphoreType.REGULAR((seq // (4 * ny),)),
+                pltpu.SemaphoreType.REGULAR((2,)),
                 dma((10,)),
                 dma, dma, dma,
                 dma((2,)),

time: 37 us -> 35.4 us (0.957)
  Pallas kernels: 36.3 us -> 34.7 us
    pallas_call x1, Pallas kernels: 36.3 us -> 34.7 us  [shards(): pl.pallas_call(body, out_shape=pltpu.VMEM((query.shape[0], columns), jnp....]
where the time goes in v5:
time: 35.4 us; the launch traced here: 35.3 us
  Pallas kernels  34.7 us (98%)
  local copies, waits for them, and re-layouts  0.58 us (2%)
    pallas_call x1, Pallas kernels, shards(): pl.pallas_call(body, out_shape=pltpu.VMEM((query.shape[0], columns), jnp....  34.7 us

profile of v5, /device:TPU:1, one launch (start us, length us, event | category | flops | bytes accessed | tf_op | source)
XLA Modules:
  0.0 35.3 jit_solution(3202038313923789260)
XLA Ops:
  0.0 34.7 %shard_map.73 = bf16[1,512]{1,0:T(2,128)(2,1)S(1)} custom-call(s32[16]{0:T(128)} %refs_0_.1, s32[16]{0:T(128)} %refs_1_.1, bf16[1,768]{1,0:T(2,128)(2,1)} %refs_2_.1, bf16[16,64,576]{2,1,0:T(8,128)(2,1)} %refs_3_.1, bf16[4,128,512]{2,1,0:T(8,128)(2,1)} %refs_4_.1, bf16[4,512,128]{2,1,0:T(8,128)(2,1)} %refs_5_.1, bf16[512,2048]{1,0:T(8,128)(2,1)} %refs_6_.1), custom_call_target="tpu_custom_call" | custom-call | tf_op jit(solution)/shard_map/pallas_call | solution.py:370
  34.7 0.6 %copy.9 = bf16[1,512]{1,0:T(2,128)(2,1)} copy(bf16[1,512]{1,0:T(2,128)(2,1)S(1)} %shard_map.73) | data formatting | bytes 2048

commit v6 on v5

--- a/solution.py
+++ b/solution.py
@@ -21,7 +21,7 @@
     owner_hbm, fill_hbm, q_hbm, cache_hbm, wuk_hbm, wuv_hbm, wout_hbm,
     out_ref,
     owner, fill, q_ref, qmine, qearly, qlate, cache, wuk, wuv, wout, bias, sel, pick, sendb, recvb, rf, xs, xr,
-    chip_in, line_in, local_sems, send1, recv1, send2, recv2, bsend, brecv, xsend, xrecv,
+    chip_in, line_in, local_sems, send1, recv1, send2, recv2, send3, recv3, bsend, brecv, xsend, xrecv,
 ):
     pages, page, width = cache.shape
     heads, nope, latent = wuk.shape
@@ -36,7 +36,8 @@
     deep = nz // 2
     late = lax.div(z, deep)
     line = z * 2 + core
-    block = lax.rem(line, 2 * deep) * ny
+    near = core * deep * ny
+    block = near + lax.rem(z, deep) * ny
     half = seq // 2
 
     def along_y(k):
@@ -63,6 +64,9 @@
             if others_only and k == 0:
                 continue
             tell(sem, peer)
+
+    def like_core(part, k):
+        return ((part * deep + lax.rem(z + k, deep)) * ny + y) * 2 + core
 
     def tell_tensor(seat):
         for k in range(1, tensor):
@@ -197,28 +201,42 @@
             mine = buf.at[pl.ds(block, ny), sent]
             pltpu.make_async_copy(mine, mine, recv1).wait()
             if part == 0:
-                send_line(0, [in_half(0, k) for k in range(1, 2 * deep)])
+                send_line(0, [like_core(0, k) for k in range(1, deep)])
                 for j in range(deep):
                     pl.semaphore_wait(chip_in.at[j], 1)
-                    send_line(0, [((deep + j) * ny + y) * 2 + c for c in range(2)])
+                    send_line(0, [((deep + j) * ny + y) * 2 + core])
                 for k in range(2 * deep):
                     tell(line_in.at[1], in_half(1, k))
             else:
-                send_line(1, [in_half(0, k) for k in range(2 * deep)])
+                send_line(1, [like_core(0, k) for k in range(deep)])
                 pl.semaphore_wait(line_in.at[1], 2 * deep)
-                send_line(1, [in_half(1, k) for k in range(1, 2 * deep)])
-
+                send_line(1, [like_core(1, k) for k in range(1, deep)])
+
+    swaps = []
     for part, buf in enumerate(queries):
-        for own, lines in ((part, 2 * deep - 1), (1 - part, 2 * deep)):
+        for own, lines in ((part, deep - 1), (1 - part, deep)):
 
             @pl.when(late == own)
             def _(part=part, buf=buf, lines=lines):
                 rest = buf.at[pl.ds(0, lines * ny), sent]
                 pltpu.make_async_copy(rest, rest, recv2.at[part]).wait()
 
+        heard = buf.at[pl.ds(near, deep * ny), sent]
+        swap = pltpu.make_async_remote_copy(
+            src_ref=heard,
+            dst_ref=heard,
+            send_sem=send3.at[part],
+            recv_sem=recv3.at[part],
+            device_id={"seq": sibling},
+            device_id_type=MESH,
+        )
+        swap.start()
+        swaps.append(swap)
+        swap.wait_recv()
+
         for p in range(pages):
             spot = owner[p] & (half - 1)
-            at = ((spot // (2 * ny)) * 2 + (spot & 1)) * ny + ((spot // 2) & (ny - 1))
+            at = ((spot & 1) * deep + spot // (2 * ny)) * ny + ((spot // 2) & (ny - 1))
             sel[p * ROWS : (p + 1) * ROWS, :] = buf[at].astype(jnp.float32)
         if part == 0:
             loads[0].wait()
@@ -345,9 +363,10 @@
         send.wait_send()
     away = qearly.at[pl.ds(0, ny - 1), sent]
     pltpu.make_async_copy(away, away, send1).wait()
-    for _ in range(2 * nz - 1):
-        away = qearly.at[pl.ds(0, ny), sent]
-        pltpu.make_async_copy(away, away, send2).wait()
+    away = qearly.at[pl.ds(0, (nz - 1) * ny), sent]
+    pltpu.make_async_copy(away, away, send2).wait()
+    for swap in swaps:
+        swap.wait_send()
     away = sendb.at[pl.ds(0, seq - 1), sent]
     pltpu.make_async_copy(away, away, bsend).wait()
 
@@ -396,6 +415,8 @@
                 dma((10,)),
                 dma, dma, dma,
                 dma((2,)),
+                dma((2,)),
+                dma((2,)),
                 dma, dma,
                 dma((tensor,)),
                 dma((tensor,)),

time: 35.4 us -> 34.8 us (0.983)
  Pallas kernels: 34.7 us -> 34 us
    pallas_call x1, Pallas kernels: 34.7 us -> 34 us  [shards(): pl.pallas_call(body, out_shape=pltpu.VMEM((query.shape[0], columns), jnp....]
where the time goes in v6:
time: 34.8 us; the launch traced here: 34.6 us
  Pallas kernels  34 us (98%)
  local copies, waits for them, and re-layouts  0.58 us (2%)
    pallas_call x1, Pallas kernels, shards(): pl.pallas_call(body, out_shape=pltpu.VMEM((query.shape[0], columns), jnp....  34 us

profile of v6, /device:TPU:1, one launch (start us, length us, event | category | flops | bytes accessed | tf_op | source)
XLA Modules:
  0.0 34.6 jit_solution(14728929351279718816)
XLA Ops:
  0.0 34.0 %shard_map.73 = bf16[1,512]{1,0:T(2,128)(2,1)S(1)} custom-call(s32[16]{0:T(128)} %refs_0_.1, s32[16]{0:T(128)} %refs_1_.1, bf16[1,768]{1,0:T(2,128)(2,1)} %refs_2_.1, bf16[16,64,576]{2,1,0:T(8,128)(2,1)} %refs_3_.1, bf16[4,128,512]{2,1,0:T(8,128)(2,1)} %refs_4_.1, bf16[4,512,128]{2,1,0:T(8,128)(2,1)} %refs_5_.1, bf16[512,2048]{1,0:T(8,128)(2,1)} %refs_6_.1), custom_call_target="tpu_custom_call" | custom-call | tf_op jit(solution)/shard_map/pallas_call | solution.py:389
  34.0 0.6 %copy.9 = bf16[1,512]{1,0:T(2,128)(2,1)} copy(bf16[1,512]{1,0:T(2,128)(2,1)S(1)} %shard_map.73) | data formatting | bytes 2048

commit v7 on v6

--- a/solution.py
+++ b/solution.py
@@ -20,7 +20,7 @@
     seq, tensor, scale, ny, nz,
     owner_hbm, fill_hbm, q_hbm, cache_hbm, wuk_hbm, wuv_hbm, wout_hbm,
     out_ref,
-    owner, fill, q_ref, qmine, qearly, qlate, cache, wuk, wuv, wout, bias, sel, pick, sendb, recvb, rf, xs, xr,
+    owner, fill, q_ref, qmine, qearly, qlate, cache, wuk, wuv, wout, vproj, bias, sel, pick, sendb, recvb, rf, xs, xr,
     chip_in, line_in, local_sems, send1, recv1, send2, recv2, send3, recv3, bsend, brecv, xsend, xrecv,
 ):
     pages, page, width = cache.shape
@@ -212,6 +212,14 @@
                 pl.semaphore_wait(line_in.at[1], 2 * deep)
                 send_line(1, [like_core(1, k) for k in range(1, deep)])
 
+    loads[1].wait()
+    loads[2].wait()
+    keys = cache[...].reshape(tokens, width)
+    for h in range(heads):
+        vproj[:, h * LANES : (h + 1) * LANES] = jnp.dot(
+            keys[:, :latent], wuv[h], preferred_element_type=jnp.float32
+        ).astype(jnp.bfloat16)
+
     swaps = []
     for part, buf in enumerate(queries):
         for own, lines in ((part, deep - 1), (1 - part, deep)):
@@ -249,8 +257,6 @@
             joined.append(jnp.concatenate([lat.astype(jnp.bfloat16), turned], axis=1))
         joined = jnp.concatenate(joined, axis=0)
 
-        if part == 0:
-            loads[1].wait()
         keys = cache[...].reshape(tokens, width)
         scores = lax.dot_general(
             joined, keys, (((1,), (1,)), ((), ())), preferred_element_type=jnp.float32
@@ -265,17 +271,11 @@
         total_hi = total.astype(jnp.bfloat16).astype(jnp.float32)
         total_lo = total - total_hi
         sums = jnp.dot(
-            weights.astype(jnp.bfloat16), keys[:, :latent], preferred_element_type=jnp.float32
+            weights.astype(jnp.bfloat16), vproj[...], preferred_element_type=jnp.float32
         )
 
-        if part == 0:
-            loads[2].wait()
         blocks = [
-            jnp.dot(
-                sums[h * pages : (h + 1) * pages].astype(jnp.bfloat16), wuv[h],
-                preferred_element_type=jnp.float32,
-            )
-            for h in range(heads)
+            sums[h * pages : (h + 1) * pages, h * LANES : (h + 1) * LANES] for h in range(heads)
         ]
         stats = jnp.zeros((pages, LANES), jnp.float32)
         for i, piece in enumerate((top_hi, top_lo, total_hi, total_lo)):
@@ -285,15 +285,6 @@
                 )
         blocks += [stats, jnp.zeros((LANES - (heads + 1) * pages, LANES), jnp.float32)]
         table = jnp.concatenate(blocks, axis=0).astype(jnp.bfloat16)
-        sendb[pl.ds(part * half, half)] = (
-            jnp.dot(
-                pick[pl.ds(part * half * ROWS, half * ROWS), :], table,
-                preferred_element_type=jnp.float32,
-            )
-            .astype(jnp.bfloat16)
-            .reshape(half, ROWS, LANES)
-        )
-
         def send_sums(k, c, base):
             peer = base + lax.rem(me + k, 2 * ny)
             pltpu.make_async_remote_copy(
@@ -307,6 +298,15 @@
             return c
 
         for level in range(part * deep, (part + 1) * deep):
+            many = 2 * ny
+            sendb[pl.ds(level * many, many)] = (
+                jnp.dot(
+                    pick[pl.ds(level * many * ROWS, many * ROWS), :], table,
+                    preferred_element_type=jnp.float32,
+                )
+                .astype(jnp.bfloat16)
+                .reshape(many, ROWS, LANES)
+            )
             lax.fori_loop(
                 jnp.where(z == level, 1, 0), 2 * ny,
                 functools.partial(send_sums, base=level * 2 * ny), 0,
@@ -402,6 +402,7 @@
                 pltpu.VMEM(w_uk.shape, w_uk.dtype),
                 pltpu.VMEM(w_uv.shape, w_uv.dtype),
                 pltpu.VMEM((tensor, w_out.shape[0], columns), w_out.dtype),
+                pltpu.VMEM((cache.shape[0] * cache.shape[1], heads * LANES), jnp.bfloat16),
                 pltpu.VMEM((page_owner.shape[0] * heads, cache.shape[0] * cache.shape[1]), jnp.float32),
                 pltpu.VMEM((page_owner.shape[0] * ROWS, LANES), jnp.float32),
                 pltpu.VMEM((seq * ROWS, LANES), jnp.bfloat16),

time: 34.8 us -> 34.4 us (0.989)
  no operation moved by 1% of the time
where the time goes in v7:
time: 34.4 us; the launch traced here: 34.3 us
  Pallas kernels  33.7 us (98%)
  local copies, waits for them, and re-layouts  0.58 us (2%)
    pallas_call x1, Pallas kernels, shards(): pl.pallas_call(body, out_shape=pltpu.VMEM((query.shape[0], columns), jnp....  33.7 us

profile of v7, /device:TPU:1, one launch (start us, length us, event | category | flops | bytes accessed | tf_op | source)
XLA Modules:
  0.0 34.3 jit_solution(14765052622872046685)
XLA Ops:
  0.0 33.7 %shard_map.73 = bf16[1,512]{1,0:T(2,128)(2,1)S(1)} custom-call(s32[16]{0:T(128)} %refs_0_.1, s32[16]{0:T(128)} %refs_1_.1, bf16[1,768]{1,0:T(2,128)(2,1)} %refs_2_.1, bf16[16,64,576]{2,1,0:T(8,128)(2,1)} %refs_3_.1, bf16[4,128,512]{2,1,0:T(8,128)(2,1)} %refs_4_.1, bf16[4,512,128]{2,1,0:T(8,128)(2,1)} %refs_5_.1, bf16[512,2048]{1,0:T(8,128)(2,1)} %refs_6_.1), custom_call_target="tpu_custom_call" | custom-call | tf_op jit(solution)/shard_map/pallas_call | solution.py:389
  33.7 0.6 %copy.9 = bf16[1,512]{1,0:T(2,128)(2,1)} copy(bf16[1,512]{1,0:T(2,128)(2,1)S(1)} %shard_map.73) | data formatting | bytes 2048

commit v8 on v7

--- a/solution.py
+++ b/solution.py
@@ -286,15 +286,19 @@
         blocks += [stats, jnp.zeros((LANES - (heads + 1) * pages, LANES), jnp.float32)]
         table = jnp.concatenate(blocks, axis=0).astype(jnp.bfloat16)
         def send_sums(k, c, base):
-            peer = base + lax.rem(me + k, 2 * ny)
-            pltpu.make_async_remote_copy(
-                src_ref=sendb.at[peer, sent],
-                dst_ref=recvb.at[me, sent],
-                send_sem=bsend,
-                recv_sem=brecv,
-                device_id={"seq": peer},
-                device_id_type=MESH,
-            ).start()
+            peer = base + k
+
+            @pl.when(peer != me)
+            def _():
+                pltpu.make_async_remote_copy(
+                    src_ref=sendb.at[peer, sent],
+                    dst_ref=recvb.at[me, sent],
+                    send_sem=bsend,
+                    recv_sem=brecv,
+                    device_id={"seq": peer},
+                    device_id_type=MESH,
+                ).start()
+
             return c
 
         for level in range(part * deep, (part + 1) * deep):
@@ -308,7 +312,7 @@
                 .reshape(many, ROWS, LANES)
             )
             lax.fori_loop(
-                jnp.where(z == level, 1, 0), 2 * ny,
+                0, 2 * ny,
                 functools.partial(send_sums, base=level * 2 * ny), 0,
             )
 

time: 34.4 us -> 34 us (0.988)
  Pallas kernels: 33.7 us -> 33.2 us
    pallas_call x1, Pallas kernels: 33.7 us -> 33.2 us  [shards(): pl.pallas_call(body, out_shape=pltpu.VMEM((query.shape[0], columns), jnp....]
where the time goes in v8:
time: 34 us; the launch traced here: 33.8 us
  Pallas kernels  33.2 us (98%)
  local copies, waits for them, and re-layouts  0.58 us (2%)
    pallas_call x1, Pallas kernels, shards(): pl.pallas_call(body, out_shape=pltpu.VMEM((query.shape[0], columns), jnp....  33.2 us

profile of v8, /device:TPU:1, one launch (start us, length us, event | category | flops | bytes accessed | tf_op | source)
XLA Modules:
  0.0 33.8 jit_solution(6453304196491388966)
XLA Ops:
  0.0 33.2 %shard_map.73 = bf16[1,512]{1,0:T(2,128)(2,1)S(1)} custom-call(s32[16]{0:T(128)} %refs_0_.1, s32[16]{0:T(128)} %refs_1_.1, bf16[1,768]{1,0:T(2,128)(2,1)} %refs_2_.1, bf16[16,64,576]{2,1,0:T(8,128)(2,1)} %refs_3_.1, bf16[4,128,512]{2,1,0:T(8,128)(2,1)} %refs_4_.1, bf16[4,512,128]{2,1,0:T(8,128)(2,1)} %refs_5_.1, bf16[512,2048]{1,0:T(8,128)(2,1)} %refs_6_.1), custom_call_target="tpu_custom_call" | custom-call | tf_op jit(solution)/shard_map/pallas_call | solution.py:393
  33.2 0.6 %copy.9 = bf16[1,512]{1,0:T(2,128)(2,1)} copy(bf16[1,512]{1,0:T(2,128)(2,1)S(1)} %shard_map.73) | data formatting | bytes 2048

commit v9 on v8

--- a/solution.py
+++ b/solution.py
@@ -40,6 +40,8 @@
     block = near + lax.rem(z, deep) * ny
     half = seq // 2
 
+    far_first = sorted(range(1, ny), key=lambda k: -min(k, ny - k))
+
     def along_y(k):
         return (z * ny + lax.rem(y + k, ny)) * 2 + core
 
@@ -80,17 +82,17 @@
 
     @pl.when(late == 0)
     def _():
-        for k in range(1, ny):
+        for k in far_first:
             tell(barrier, along_y(k))
+        tell_tensor(me)
         tell_half(barrier, 0, True)
         for k in range(deep):
             tell(barrier, (deep + lax.rem(z + k, deep)) * 2 * ny + y * 2)
-        tell_tensor(me)
 
     @pl.when(late == 1)
     def _():
         tell(barrier, sibling)
-        for k in range(1, ny):
+        for k in far_first:
             tell(barrier, along_y(k) + 1 - core)
         tell_tensor(first_core + 1)
 
@@ -140,7 +142,7 @@
         @pl.when(late == part)
         def _(buf=buf):
             mine = buf.at[pl.ds(block + y, 1), sent]
-            for k in range(1, ny):
+            for k in far_first:
                 pltpu.make_async_remote_copy(
                     src_ref=qmine.at[:, sent],
                     dst_ref=mine,

time: 34 us -> 33.9 us (level)
  no operation moved by 1% of the time
where the time goes in v9:
time: 33.9 us; the launch traced here: 33.7 us
  Pallas kernels  33.1 us (98%)
  local copies, waits for them, and re-layouts  0.58 us (2%)
    pallas_call x1, Pallas kernels, shards(): pl.pallas_call(body, out_shape=pltpu.VMEM((query.shape[0], columns), jnp....  33.1 us

profile of v9, /device:TPU:1, one launch (start us, length us, event | category | flops | bytes accessed | tf_op | source)
XLA Modules:
  0.0 33.7 jit_solution(15825409344118356009)
XLA Ops:
  0.0 33.1 %shard_map.73 = bf16[1,512]{1,0:T(2,128)(2,1)S(1)} custom-call(s32[16]{0:T(128)} %refs_0_.1, s32[16]{0:T(128)} %refs_1_.1, bf16[1,768]{1,0:T(2,128)(2,1)} %refs_2_.1, bf16[16,64,576]{2,1,0:T(8,128)(2,1)} %refs_3_.1, bf16[4,128,512]{2,1,0:T(8,128)(2,1)} %refs_4_.1, bf16[4,512,128]{2,1,0:T(8,128)(2,1)} %refs_5_.1, bf16[512,2048]{1,0:T(8,128)(2,1)} %refs_6_.1), custom_call_target="tpu_custom_call" | custom-call | tf_op jit(solution)/shard_map/pallas_call | solution.py:395
  33.1 0.6 %copy.9 = bf16[1,512]{1,0:T(2,128)(2,1)} copy(bf16[1,512]{1,0:T(2,128)(2,1)S(1)} %shard_map.73) | data formatting | bytes 2048

commit v10 on v9

--- a/solution.py
+++ b/solution.py
@@ -203,8 +203,9 @@
             mine = buf.at[pl.ds(block, ny), sent]
             pltpu.make_async_copy(mine, mine, recv1).wait()
             if part == 0:
-                send_line(0, [like_core(0, k) for k in range(1, deep)])
                 for j in range(deep):
+                    if j == deep - 1:
+                        send_line(0, [like_core(0, k) for k in range(1, deep)])
                     pl.semaphore_wait(chip_in.at[j], 1)
                     send_line(0, [((deep + j) * ny + y) * 2 + core])
                 for k in range(2 * deep):

time: 33.9 us -> 33.9 us (level)
  no operation moved by 1% of the time
where the time goes in v10:
time: 33.9 us; the launch traced here: 33.7 us
  Pallas kernels  33.1 us (98%)
  local copies, waits for them, and re-layouts  0.58 us (2%)
    pallas_call x1, Pallas kernels, shards(): pl.pallas_call(body, out_shape=pltpu.VMEM((query.shape[0], columns), jnp....  33.1 us

profile of v10, /device:TPU:1, one launch (start us, length us, event | category | flops | bytes accessed | tf_op | source)
XLA Modules:
  0.0 33.7 jit_solution(13102461431001268679)
XLA Ops:
  0.0 33.1 %shard_map.73 = bf16[1,512]{1,0:T(2,128)(2,1)S(1)} custom-call(s32[16]{0:T(128)} %refs_0_.1, s32[16]{0:T(128)} %refs_1_.1, bf16[1,768]{1,0:T(2,128)(2,1)} %refs_2_.1, bf16[16,64,576]{2,1,0:T(8,128)(2,1)} %refs_3_.1, bf16[4,128,512]{2,1,0:T(8,128)(2,1)} %refs_4_.1, bf16[4,512,128]{2,1,0:T(8,128)(2,1)} %refs_5_.1, bf16[512,2048]{1,0:T(8,128)(2,1)} %refs_6_.1), custom_call_target="tpu_custom_call" | custom-call | tf_op jit(solution)/shard_map/pallas_call | solution.py:396
  33.1 0.6 %copy.9 = bf16[1,512]{1,0:T(2,128)(2,1)} copy(bf16[1,512]{1,0:T(2,128)(2,1)S(1)} %shard_map.73) | data formatting | bytes 2048
